TPU v7x, 512 devices: a whole 4x4x16 slice. The times are simulated.
512 devices in a mesh: dp: 16 (over x_hi, y, core), seq: 32 (over x_lo, z).
Axes of the slice: x: 4 (x_hi: 2, x_lo: 2; x = x_hi * 2 + x_lo), y: 4, z: 16, core: 2. Of those that a mesh axis runs over, the one named last changes fastest.
Arguments:
- queries: bfloat16 [16, 32768, 128], P('dp', 'seq'), may hold values from -6 to 6
- key_vectors: bfloat16 [16, 32768, 128], P('dp', 'seq'), may hold values from -6 to 6
- value_vectors: bfloat16 [16, 32768, 128], P('dp', 'seq'), may hold values from -6 to 6
- out_grad: bfloat16 [16, 32768, 128], P('dp', 'seq'), may hold values from -6 to 6
- log_decay: float32 [16, 1, 32768], P('dp', None, 'seq'), may hold values from -0.8 to 0, as said below
- prev_grads: bfloat16 [16, 1024, 6144], P('dp', 'seq'), may hold values from -6 to 6
Outputs:
- attn_out: bfloat16 [16, 32768, 128], P('dp', 'seq')
- grad_query: bfloat16 [16, 32768, 128], P('dp', 'seq')
- grad_key: bfloat16 [16, 32768, 128], P('dp', 'seq')
- grad_value: bfloat16 [16, 32768, 128], P('dp', 'seq')
- grad_shard: float32 [1024, 6144], P('seq', 'dp')
Inputs may be any that keep to these rules, and one draw needn't show every extreme that they name: `log_decay`: every entry is negative.
All inputs are finite; a program needn't handle non-finite values.
Results may differ from a plain program's by a relative error of at most 0.012.
Values may be sent and summed in bfloat16 or wider, within the bound.
A program may use at most 64 MiB of HBM per device.

v0:
```python
import jax
import jax.numpy as jnp
from jax import lax
from jax.sharding import PartitionSpec as P

BLK = 512
NORM_EPS = 1e-06
FULL_PRECISION = lax.Precision.HIGHEST


def product(left, right):
    return jnp.dot(left, right, precision=FULL_PRECISION, preferred_element_type=jnp.float32)


def decay_mask(running):
    spread = running[:, None] - running[None, :]
    lower_mask = jnp.tril(jnp.ones(spread.shape, dtype=bool))
    return jnp.where(lower_mask, jnp.exp(jnp.minimum(spread, 0.0)), 0.0)


def forward_local(query_head, key_head, value_head, decay_head):
    head_width = query_head.shape[-1]

    def advance(carried, block_inputs):
        query_block, key_block, value_block, decay_block = block_inputs
        running = jnp.cumsum(decay_block)
        scores = jnp.dot(query_block, key_block.T, preferred_element_type=jnp.float32) * decay_mask(
            running
        )
        query_wide = query_block.astype(jnp.float32)
        key_wide = key_block.astype(jnp.float32)
        value_wide = value_block.astype(jnp.float32)
        block_out = product(scores, value_wide) + jnp.exp(running)[:, None] * product(
            query_wide, carried
        )
        weights = jnp.exp(running[-1] - running)
        updated = jnp.exp(running[-1]) * carried + product(
            (key_wide * weights[:, None]).T, value_wide
        )
        return (updated, (block_out, carried))

    return lax.scan(
        advance,
        jnp.zeros((head_width, head_width), jnp.float32),
        (query_head, key_head, value_head, decay_head),
    )


def backward_local(query_head, key_head, value_head, dattn_head, decay_head, start_head):
    head_width = query_head.shape[-1]

    def retreat(later_sum, block_inputs):
        query_block, key_block, value_block, dattn_block, decay_block, carried = block_inputs
        running = jnp.cumsum(decay_block)
        decay_weights = decay_mask(running)
        scores = (
            jnp.dot(query_block, key_block.T, preferred_element_type=jnp.float32) * decay_weights
        )
        query_wide = query_block.astype(jnp.float32)
        key_wide = key_block.astype(jnp.float32)
        value_wide = value_block.astype(jnp.float32)
        dscores = product(dattn_block, value_wide.T) * decay_weights
        lead_decay = jnp.exp(running)[:, None]
        tail_decay = jnp.exp(running[-1] - running)[:, None]
        grad_q = product(dscores, key_wide) + lead_decay * product(dattn_block, carried.T)
        grad_k = product(dscores.T, query_wide) + tail_decay * product(value_wide, later_sum.T)
        grad_v = product(scores.T, dattn_block) + tail_decay * product(key_wide, later_sum)
        updated = jnp.exp(running[-1]) * later_sum + product(
            (query_wide * lead_decay).T, dattn_block
        )
        return (updated, (grad_q, grad_k, grad_v))

    return lax.scan(
        retreat,
        jnp.zeros((head_width, head_width), jnp.float32),
        (query_head, key_head, value_head, dattn_head, decay_head, start_head),
        reverse=True,
    )


def weigh_fold(block_logs, own_index, upward, running_sum, shard_part):
    summed_logs = jnp.cumsum(block_logs, axis=0)
    own_cum = lax.dynamic_index_in_dim(summed_logs, own_index, 0, keepdims=False)
    own_log = lax.dynamic_index_in_dim(block_logs, own_index, 0, keepdims=False)
    piece_count = shard_part.shape[0]
    token_offsets = jnp.arange(piece_count, dtype=jnp.int32)
    if upward:
        spread = summed_logs - block_logs - own_cum[None, :]
        usable = token_offsets > own_index
    else:
        spread = own_cum[None, :] - own_log[None, :] - summed_logs
        usable = token_offsets < own_index
    weights = jnp.where(usable[:, None], jnp.exp(jnp.minimum(spread, 0.0)), 0.0)
    return running_sum + jnp.einsum("nh,nhab->hab", weights, shard_part, precision=FULL_PRECISION)


def local(queries, key_vectors, value_vectors, out_grad, log_decay, prev_grads):
    row_count = queries.shape[1]
    head_count = log_decay.shape[1]
    head_width = queries.shape[2] // head_count
    block_count = row_count // BLK

    def by_head(tensor):
        return tensor[0].reshape(row_count, head_count, head_width).transpose(1, 0, 2)

    def by_block(tensor):
        return tensor.reshape(head_count, block_count, BLK, head_width)

    def to_rows(tensor):
        return (
            tensor.transpose(1, 0, 2)
            .reshape(1, row_count, head_count * head_width)
            .astype(jnp.bfloat16)
        )

    query_heads = by_head(queries)
    key_heads = by_head(key_vectors)
    value_heads = by_head(value_vectors)
    decay_rows = log_decay[0]
    decay_blocks = decay_rows.reshape(head_count, block_count, BLK)
    cumulative = jnp.cumsum(decay_rows, axis=1)
    log_total = cumulative[:, -1]
    local_state, (local_out, block_starts) = jax.vmap(forward_local)(
        by_block(query_heads), by_block(key_heads), by_block(value_heads), decay_blocks
    )
    identity = (
        jnp.zeros((head_count,), jnp.float32),
        jnp.zeros((head_count, head_width, head_width), jnp.float32),
    )
    own_index = lax.axis_index("seq")
    block_logs = lax.all_gather(log_total[None], "seq", axis=0, tiled=True)
    incoming = weigh_fold(
        block_logs,
        own_index,
        False,
        identity[1],
        lax.all_gather(local_state[None].astype(jnp.bfloat16), "seq", axis=0, tiled=True).astype(
            jnp.float32
        ),
    )
    query_wide = query_heads.astype(jnp.float32)
    key_wide = key_heads.astype(jnp.float32)
    value_wide = value_heads.astype(jnp.float32)
    lead_decay = jnp.exp(cumulative)[:, :, None]
    attention = local_out.reshape(head_count, row_count, head_width) + lead_decay * jnp.einsum(
        "hta,hab->htb", query_wide, incoming, precision=FULL_PRECISION
    )
    norm_ratio = lax.rsqrt(jnp.mean(attention * attention, axis=-1, keepdims=True) + NORM_EPS)
    attn_out = to_rows(attention * norm_ratio)
    cotangent = by_head(out_grad).astype(jnp.float32)
    cubed = norm_ratio * norm_ratio * norm_ratio
    dattn = (
        norm_ratio * cotangent
        - cubed / head_width * jnp.sum(cotangent * attention, axis=-1, keepdims=True) * attention
    )
    local_future, (grad_q_local, grad_k_local, grad_v_local) = jax.vmap(backward_local)(
        by_block(query_heads),
        by_block(key_heads),
        by_block(value_heads),
        by_block(dattn),
        decay_blocks,
        block_starts,
    )
    outgoing = weigh_fold(
        block_logs,
        own_index,
        True,
        identity[1],
        lax.all_gather(local_future[None].astype(jnp.bfloat16), "seq", axis=0, tiled=True).astype(
            jnp.float32
        ),
    )
    tail_decay = jnp.exp(log_total[:, None] - cumulative)[:, :, None]
    grad_query = grad_q_local.reshape(head_count, row_count, head_width) + lead_decay * jnp.einsum(
        "htb,hab->hta", dattn, incoming, precision=FULL_PRECISION
    )
    grad_key = grad_k_local.reshape(head_count, row_count, head_width) + tail_decay * jnp.einsum(
        "htb,hab->hta", value_wide, outgoing, precision=FULL_PRECISION
    )
    grad_value = grad_v_local.reshape(head_count, row_count, head_width) + tail_decay * jnp.einsum(
        "hta,hab->htb", key_wide, outgoing, precision=FULL_PRECISION
    )
    summed = lax.psum_scatter(
        prev_grads.astype(jnp.float32).astype(jnp.bfloat16), "dp", scatter_dimension=2, tiled=True
    ).astype(jnp.float32)
    return (attn_out, to_rows(grad_query), to_rows(grad_key), to_rows(grad_value), summed[0])


def solution(mesh):
    return jax.shard_map(
        local,
        mesh=mesh,
        in_specs=(
            P("dp", "seq", None),
            P("dp", "seq", None),
            P("dp", "seq", None),
            P("dp", "seq", None),
            P("dp", None, "seq"),
            P("dp", "seq", None),
        ),
        out_specs=(
            P("dp", "seq", None),
            P("dp", "seq", None),
            P("dp", "seq", None),
            P("dp", "seq", None),
            P("seq", "dp"),
        ),
        check_vma=False,
    )
```

profile of v0, /device:TPU:8, one launch (start us, length us, event | category | flops | bytes accessed | tf_op | source)
XLA Modules:
  0.0 324.7 jit_solution(16678804130265049411)
XLA Ops:
  8.1 15.7 %while.36 = (s32[]{:T(128)}, f32[1,128,128]{2,1,0:T(8,128)S(1)}, f32[2,1,512,128]{3,2,1,0:T(8,128)S(1)}, f32[2,1,128,128]{3,2,1,0:T(8,128)S(1)}, f32[2,1,512]{2,...) while((s32[]{:T(128)}, f32[1,128,128]{2,1,0:T(8,128)S(1)}, ...), condition=%wide.region_3.4_spmd.clone, body=%wide.region_0.3_spmd.clone.sunk | while | flops 672809472 | bytes 7176599 | solution.py:42
  8.2 0.8 constant_dynamic-slice_fusion.5
  12.3 1.3 convolution_multiply_fusion.14
  13.6 1.5 fusion.176
  16.0 0.8 constant_dynamic-slice_fusion.5
  20.1 1.3 convolution_multiply_fusion.14
  21.4 1.5 fusion.176
  24.6 6.1 %copy.49 = bf16[1,32,6144]{1,0,2:T(2,128)(2,1)S(1)} copy(bf16[1,32,6144]{2,1,0:T(8,128)(2,1)} %param.15) | data formatting | bytes 786432
  30.7 1.4 copy.57
  34.1 1.3 dynamic-slice
  37.4 70.7 %all-reduce = f32[32]{0:T(128)S(1)} all-reduce(f32[32]{0:T(128)S(1)} %bitcast_dynamic-update-slice_fusion.1), channel_id=1, replica_groups=mesh['dp'=16,'seq'=32] {'seq'}, use_global_device_ids=true, to_apply=%add | all-reduce | flops 32 | bytes 256
  108.8 1.1 copy.33
  109.9 1.2 copy.45
  111.2 1.2 fusion.120
  112.4 2.0 select_reduce_fusion
  114.4 46.8 %all-gather.5.cloned.1.call-done = bf16[32,128,128]{2,1,0:T(8,128)(2,1)} async-done(((bf16[1,128,128]{2,1,0:T(8,128)(2,1)}), bf16[32,128,128]{2,1,0:T(8,128)(2,1)}) %all-gather.5.cloned.1.call-update) | async-done | bytes 1048592 | tf_op jit(solution)/shard_map/all_gather | solution.py:137
  161.2 2.2 fusion.105
  164.4 0.8 broadcast.304
  165.2 21.6 %while.37 = (s32[]{:T(128)}, f32[1,128,128]{2,1,0:T(8,128)S(1)}, f32[2,1,512,128]{3,2,1,0:T(8,128)}, f32[2,1,512,128]{3,2,1,0:T(8,128)S(1)}, f32[2,1,512,128]{3,...) while((s32[]{:T(128)}, f32[1,128,128]{2,1,0:T(8,128)S(1)}, ...), condition=%wide.region_12.13_spmd.clone, body=%wide.region_9.12_spmd.clone.sunk | while | flops 2083668480 | bytes 14791102 | solution.py:73
  167.0 0.7 slice_bitcast_fusion.6
  170.4 1.0 fusion.199
  173.1 1.8 fusion.201
  177.8 0.7 slice_bitcast_fusion.6
  181.2 1.0 fusion.199
  183.9 1.8 fusion.201
  187.5 1.0 reshape_bitcast_fusion
  190.0 0.8 copy.38
  191.2 1.7 fusion.102
  193.0 119.5 %all-gather.7.cloned.1.call-done = bf16[32,128,128]{2,1,0:T(8,128)(2,1)} async-done(((bf16[1,128,128]{2,1,0:T(8,128)(2,1)}), bf16[32,128,128]{2,1,0:T(8,128)(2,1)}) %all-gather.7.cloned.1.call-update) | async-done | bytes 1048592 | tf_op jit(solution)/shard_map/all_gather | solution.py:169
  312.5 2.2 fusion.103
  315.2 0.8 copy.40
  316.4 0.8 copy.39
  (142 shorter events, 25.8 us)
Async XLA Ops:
  8.0 153.2 %all-gather.5.cloned.1.call-start = ((), (), s32[]{:S(2)}) async-start(), calls=%async_computation.1 | async-start | bytes 1081344 | tf_op jit(solution)/shard_map/all_gather | solution.py:137
  8.1 7.0 %copy-start.4 = (bf16[2,1,512,128]{3,2,1,0:T(8,128)(2,1)S(1)}, bf16[2,1,512,128]{3,2,1,0:T(8,128)(2,1)}, u32[]{:S(2)}) copy-start(bf16[2,1,512,128]{3,2,1,0:T(8,128)(2,1)} %get-tuple-element.592) | copy-start | bytes 786436 | tf_op jit(solution)/shard_map/vmap()/while
  8.1 7.2 %copy-start = (bf16[2,1,512,128]{3,2,1,0:T(8,128)(2,1)S(1)}, bf16[2,1,512,128]{3,2,1,0:T(8,128)(2,1)}, u32[]{:S(2)}) copy-start(bf16[2,1,512,128]{3,2,1,0:T(8,128)(2,1)} %get-tuple-element.590) | copy-start | bytes 786436 | tf_op jit(solution)/shard_map/vmap()/while
  8.1 7.2 %copy-start.2 = (bf16[2,1,512,128]{3,2,1,0:T(8,128)(2,1)S(1)}, bf16[2,1,512,128]{3,2,1,0:T(8,128)(2,1)}, u32[]{:S(2)}) copy-start(bf16[2,1,512,128]{3,2,1,0:T(8,128)(2,1)} %get-tuple-element.591) | copy-start | bytes 786436 | tf_op jit(solution)/shard_map/vmap()/while
  16.0 7.0 %copy-start.4 = (bf16[2,1,512,128]{3,2,1,0:T(8,128)(2,1)S(1)}, bf16[2,1,512,128]{3,2,1,0:T(8,128)(2,1)}, u32[]{:S(2)}) copy-start(bf16[2,1,512,128]{3,2,1,0:T(8,128)(2,1)} %get-tuple-element.592) | copy-start | bytes 786436 | tf_op jit(solution)/shard_map/vmap()/while
  16.0 7.3 %copy-start = (bf16[2,1,512,128]{3,2,1,0:T(8,128)(2,1)S(1)}, bf16[2,1,512,128]{3,2,1,0:T(8,128)(2,1)}, u32[]{:S(2)}) copy-start(bf16[2,1,512,128]{3,2,1,0:T(8,128)(2,1)} %get-tuple-element.590) | copy-start | bytes 786436 | tf_op jit(solution)/shard_map/vmap()/while
  16.0 7.2 %copy-start.2 = (bf16[2,1,512,128]{3,2,1,0:T(8,128)(2,1)S(1)}, bf16[2,1,512,128]{3,2,1,0:T(8,128)(2,1)}, u32[]{:S(2)}) copy-start(bf16[2,1,512,128]{3,2,1,0:T(8,128)(2,1)} %get-tuple-element.591) | copy-start | bytes 786436 | tf_op jit(solution)/shard_map/vmap()/while
  23.8 0.8 copy-start.9
  23.8 6.9 %copy-start.10 = (f32[2,1,128,128]{3,2,1,0:T(8,128)}, f32[2,1,128,128]{3,2,1,0:T(8,128)S(1)}, u32[]{:S(2)}) copy-start(f32[2,1,128,128]{3,2,1,0:T(8,128)S(1)} %get-tuple-element.606) | copy-start | bytes 393220
  24.6 162.9 %reduce-scatter.4.cloned.1.call-start = ((), (), s32[]{:S(2)}) async-start(), calls=%async_computation.3 | async-start | bytes 1671168
  30.7 1.5 copy-start.12
  32.1 131.3 %copy-start.5 = (bf16[2,1,512,128]{3,2,1,0:T(8,128)(2,1)S(1)}, bf16[2,1,512,128]{3,2,1,0:T(8,128)(2,1)}, u32[]{:S(2)}) copy-start(bf16[2,1,512,128]{3,2,1,0:T(8,128)(2,1)} %get-tuple-element.645) | copy-start | bytes 786436
  32.1 280.4 %all-gather.7.cloned.1.call-start = ((), (), s32[]{:S(2)}) async-start(), calls=%async_computation.2 | async-start | bytes 1081344 | tf_op jit(solution)/shard_map/all_gather | solution.py:169
  108.1 55.9 %copy-start.13 = (f32[1024]{0:T(1024)}, f32[1024]{0:T(1024)S(1)}, u32[]{:S(2)}) copy-start(f32[1024]{0:T(1024)S(1)} %get-tuple-element.432) | copy-start | bytes 12292
  163.3 1.9 copy-start.1
  163.4 1.8 copy-start.3
  163.9 1.3 copy-start.15
  167.0 5.1 %copy-start.6 = (f32[2,1,512,128]{3,2,1,0:T(8,128)S(1)}, f32[2,1,512,128]{3,2,1,0:T(8,128)}, u32[]{:S(2)}) copy-start(f32[2,1,512,128]{3,2,1,0:T(8,128)} %get-tuple-element.612) | copy-start | bytes 1572868 | tf_op jit(solution)/shard_map/vmap()/while
  167.0 5.1 %copy-start.11 = (f32[2,1,128,128]{3,2,1,0:T(8,128)S(1)}, f32[2,1,128,128]{3,2,1,0:T(8,128)}, u32[]{:S(2)}) copy-start(f32[2,1,128,128]{3,2,1,0:T(8,128)} %get-tuple-element.634) | copy-start | bytes 393220 | tf_op jit(solution)/shard_map/vmap()/while
  172.5 3.5 %copy-start.7 = (f32[2,1,512,128]{3,2,1,0:T(8,128)}, f32[2,1,512,128]{3,2,1,0:T(8,128)S(1)}, u32[]{:S(2)}) copy-start(f32[2,1,512,128]{3,2,1,0:T(8,128)S(1)} %fusion.198) | copy-start | bytes 1572868 | tf_op jit(solution)/shard_map/vmap()/while
  177.8 5.1 %copy-start.6 = (f32[2,1,512,128]{3,2,1,0:T(8,128)S(1)}, f32[2,1,512,128]{3,2,1,0:T(8,128)}, u32[]{:S(2)}) copy-start(f32[2,1,512,128]{3,2,1,0:T(8,128)} %get-tuple-element.612) | copy-start | bytes 1572868 | tf_op jit(solution)/shard_map/vmap()/while
  177.8 5.1 %copy-start.11 = (f32[2,1,128,128]{3,2,1,0:T(8,128)S(1)}, f32[2,1,128,128]{3,2,1,0:T(8,128)}, u32[]{:S(2)}) copy-start(f32[2,1,128,128]{3,2,1,0:T(8,128)} %get-tuple-element.634) | copy-start | bytes 393220 | tf_op jit(solution)/shard_map/vmap()/while
  183.3 3.5 %copy-start.7 = (f32[2,1,512,128]{3,2,1,0:T(8,128)}, f32[2,1,512,128]{3,2,1,0:T(8,128)S(1)}, u32[]{:S(2)}) copy-start(f32[2,1,512,128]{3,2,1,0:T(8,128)S(1)} %fusion.198) | copy-start | bytes 1572868 | tf_op jit(solution)/shard_map/vmap()/while
  186.8 4.4 %copy-start.8 = (f32[2,1,512,128]{3,2,1,0:T(8,128)S(1)}, f32[2,1,512,128]{3,2,1,0:T(8,128)}, u32[]{:S(2)}) copy-start(f32[2,1,512,128]{3,2,1,0:T(8,128)} %get-tuple-element.272) | copy-start | bytes 1572868
  186.8 4.4 %copy-start.14 = (f32[1024]{0:T(1024)S(1)}, f32[1024]{0:T(1024)}, u32[]{:S(2)}) copy-start(f32[1024]{0:T(1024)} %copy-done.13) | copy-start | bytes 12292
  186.8 125.7 %copy-start.16 = (f32[32]{0:T(128)S(1)}, f32[32]{0:T(128)}, u32[]{:S(2)}) copy-start(f32[32]{0:T(128)} %get-tuple-element.387) | copy-start | bytes 388
Sparse Core Ops, SparseCore 0:
  24.6 136.4 all-gather.4
  187.6 124.8 all-gather.6
Sparse Core Ops, SparseCore 1:
  32.2 96.2 reduce-scatter.3
where the time goes:
time: 326 us; the launch traced here: 325 us
  waiting for transfers between devices  166 us (51%)
  blocking collectives  70.7 us (22%)
  local copies, waits for them, and re-layouts  27.9 us (9%)
  matrix products  26.8 us (8%)
  between operations  17.1 us (5%)
  other arithmetic  9.85 us (3%)
  loops' own time  5.81 us (2%)
    all_gather x1, waiting for transfers between devices, local(): lax.all_gather(local_future[None].astype(jnp.bfloat16), 'seq', axis=0, ti...  120 us
    unnamed x1, blocking collectives  70.7 us
    all_gather x1, waiting for transfers between devices, local(): lax.all_gather(local_state[None].astype(jnp.bfloat16), 'seq', axis=0, til...  46.8 us
    dot_general x22, matrix products, product(): jnp.dot(left, right, precision=FULL_PRECISION, preferred_element_type=jnp...  16.3 us
    unnamed x36, local copies, waits for them, and re-layouts  15.1 us
  transfers between devices with their start and end apart: 3, of which 2 were waited for; matrix products, arithmetic and copies ran while one was open for 14% of the time, Pallas kernels for 0%

commit v1 on v0

--- a/solution.py
+++ b/solution.py
@@ -134,9 +134,15 @@
         own_index,
         False,
         identity[1],
-        lax.all_gather(local_state[None].astype(jnp.bfloat16), "seq", axis=0, tiled=True).astype(
-            jnp.float32
-        ),
+        jnp.concatenate(
+            lax.all_to_all(
+                jnp.stack([local_state[None].astype(jnp.bfloat16)] * lax.axis_size("seq")),
+                "seq",
+                0,
+                0,
+            ),
+            axis=0,
+        ).astype(jnp.float32),
     )
     query_wide = query_heads.astype(jnp.float32)
     key_wide = key_heads.astype(jnp.float32)

time: 326 us -> 315 us (0.966)
  waiting for transfers between devices: 166 us -> 120 us
  blocking collectives: 70.7 us -> 89.6 us
  starting transfers between devices: 0.08 us -> 16.6 us
    all_gather x1 -> x0, waiting for transfers between devices: 46.8 us -> none  [local(): lax.all_gather(local_state[None].astype(jnp.bfloat16), 'seq', axis=0, til...]
    unnamed x1, blocking collectives: 70.7 us -> 89.6 us
    all_to_all x0 -> x1, starting transfers between devices: none -> 16.5 us  [local(): lax.all_to_all(jnp.stack([local_state[None].astype(jnp.bfloat16)] * lax.a...]
    unnamed x36 -> x38, local copies, waits for them, and re-layouts: 15.1 us -> 14.1 us
  transfers between devices with their start and end apart: 3 -> 3, of which waited for: 2 -> 1; matrix products, arithmetic and copies ran while one was open for 14% -> 15% of each run, Pallas kernels for 0% -> 0%
where the time goes in v1:
time: 315 us; the launch traced here: 314 us
  waiting for transfers between devices  120 us (38%)
  blocking collectives  89.6 us (28%)
  local copies, waits for them, and re-layouts  28.3 us (9%)
  matrix products  26.9 us (9%)
  between operations  17.1 us (5%)
  starting transfers between devices  16.6 us (5%)
  other arithmetic  9.27 us (3%)
  loops' own time  5.89 us (2%)
    all_gather x1, waiting for transfers between devices, local(): lax.all_gather(local_future[None].astype(jnp.bfloat16), 'seq', axis=0, ti...  120 us
    unnamed x1, blocking collectives  89.6 us
    all_to_all x1, starting transfers between devices, local(): lax.all_to_all(jnp.stack([local_state[None].astype(jnp.bfloat16)] * lax.a...  16.5 us
    dot_general x22, matrix products, product(): jnp.dot(left, right, precision=FULL_PRECISION, preferred_element_type=jnp...  16.3 us
    unnamed x38, local copies, waits for them, and re-layouts  14.1 us
  transfers between devices with their start and end apart: 3, of which 1 were waited for; matrix products, arithmetic and copies ran while one was open for 15% of the time, Pallas kernels for 0%

profile of v1, /device:TPU:8, one launch (start us, length us, event | category | flops | bytes accessed | tf_op | source)
XLA Modules:
  0.0 313.6 jit_solution(13078067399122757379)
XLA Ops:
  8.1 15.7 %while.36 = (s32[]{:T(128)}, f32[1,128,128]{2,1,0:T(8,128)S(1)}, f32[2,1,512,128]{3,2,1,0:T(8,128)S(1)}, f32[2,1,128,128]{3,2,1,0:T(8,128)S(1)}, f32[2,1,512]{2,...) while((s32[]{:T(128)}, f32[1,128,128]{2,1,0:T(8,128)S(1)}, ...), condition=%wide.region_3.4_spmd.clone, body=%wide.region_0.3_spmd.clone.sunk | while | flops 672809472 | bytes 7176599 | solution.py:42
  8.1 0.8 constant_dynamic-slice_fusion.5
  12.2 1.3 convolution_multiply_fusion.14
  13.5 1.5 fusion.176
  15.9 0.8 constant_dynamic-slice_fusion.5
  20.1 1.3 convolution_multiply_fusion.14
  21.3 1.5 fusion.176
  23.8 1.2 stack.2
  25.0 16.5 %all-to-all-start = ((bf16[32,1,1,128,128]{4,3,2,1,0:T(8,128)(2,1)}), bf16[32,1,1,128,128]{4,3,2,1,0:T(8,128)(2,1)}, u32[]{:S(2)}, u32[]{:S(2)}) async-start(bf16[32,1,1,128,128]{4,3,2,1,0:T(8,128)(2,1)} %stack.2), calls=%async_computation | async-start | bytes 2097152 | tf_op jit(solution)/shard_map/all_to_all | solution.py:138
  41.6 6.1 %copy.49 = bf16[1,32,6144]{1,0,2:T(2,128)(2,1)S(1)} copy(bf16[1,32,6144]{2,1,0:T(8,128)(2,1)} %param.15) | data formatting | bytes 786432
  47.8 1.4 copy.57
  51.1 1.3 dynamic-slice
  54.4 89.6 %all-reduce = f32[32]{0:T(128)S(1)} all-reduce(f32[32]{0:T(128)S(1)} %bitcast_dynamic-update-slice_fusion.1), channel_id=1, replica_groups=mesh['dp'=16,'seq'=32] {'seq'}, use_global_device_ids=true, to_apply=%add | all-reduce | flops 32 | bytes 256
  144.9 1.2 copy.45
  146.2 1.2 fusion.120
  147.3 1.9 select_reduce_fusion
  149.3 2.2 fusion.105
  152.5 0.8 broadcast.306
  153.4 22.1 %while.37 = (s32[]{:T(128)}, f32[1,128,128]{2,1,0:T(8,128)S(1)}, f32[2,1,512,128]{3,2,1,0:T(8,128)}, f32[2,1,512,128]{3,2,1,0:T(8,128)S(1)}, f32[2,1,512,128]{3,...) while((s32[]{:T(128)}, f32[1,128,128]{2,1,0:T(8,128)S(1)}, ...), condition=%wide.region_12.13_spmd.clone, body=%wide.region_9.12_spmd.clone.sunk | while | flops 2083668480 | bytes 14791102 | solution.py:73
  154.5 0.8 reduce-window.55
  158.9 1.0 fusion.199
  161.6 1.8 fusion.201
  165.5 0.8 reduce-window.55
  169.9 1.0 fusion.199
  172.6 1.8 fusion.201
  176.2 1.0 reshape_bitcast_fusion
  178.6 0.8 copy.38
  179.9 1.7 fusion.102
  181.6 119.8 %all-gather.3.cloned.1.call-done = bf16[32,128,128]{2,1,0:T(8,128)(2,1)} async-done(((bf16[1,128,128]{2,1,0:T(8,128)(2,1)}), bf16[32,128,128]{2,1,0:T(8,128)(2,1)}) %all-gather.3.cloned.1.call-update) | async-done | bytes 1048592 | tf_op jit(solution)/shard_map/all_gather | solution.py:175
  301.5 2.2 fusion.103
  304.1 0.8 copy.40
  305.3 0.8 copy.39
  (144 shorter events, 25.4 us)
Async XLA Ops:
  8.1 7.0 %copy-start.4 = (bf16[2,1,512,128]{3,2,1,0:T(8,128)(2,1)S(1)}, bf16[2,1,512,128]{3,2,1,0:T(8,128)(2,1)}, u32[]{:S(2)}) copy-start(bf16[2,1,512,128]{3,2,1,0:T(8,128)(2,1)} %get-tuple-element.592) | copy-start | bytes 786436 | tf_op jit(solution)/shard_map/vmap()/while
  8.1 7.2 %copy-start = (bf16[2,1,512,128]{3,2,1,0:T(8,128)(2,1)S(1)}, bf16[2,1,512,128]{3,2,1,0:T(8,128)(2,1)}, u32[]{:S(2)}) copy-start(bf16[2,1,512,128]{3,2,1,0:T(8,128)(2,1)} %get-tuple-element.590) | copy-start | bytes 786436 | tf_op jit(solution)/shard_map/vmap()/while
  8.1 7.2 %copy-start.2 = (bf16[2,1,512,128]{3,2,1,0:T(8,128)(2,1)S(1)}, bf16[2,1,512,128]{3,2,1,0:T(8,128)(2,1)}, u32[]{:S(2)}) copy-start(bf16[2,1,512,128]{3,2,1,0:T(8,128)(2,1)} %get-tuple-element.591) | copy-start | bytes 786436 | tf_op jit(solution)/shard_map/vmap()/while
  15.9 7.0 %copy-start.4 = (bf16[2,1,512,128]{3,2,1,0:T(8,128)(2,1)S(1)}, bf16[2,1,512,128]{3,2,1,0:T(8,128)(2,1)}, u32[]{:S(2)}) copy-start(bf16[2,1,512,128]{3,2,1,0:T(8,128)(2,1)} %get-tuple-element.592) | copy-start | bytes 786436 | tf_op jit(solution)/shard_map/vmap()/while
  15.9 7.2 %copy-start = (bf16[2,1,512,128]{3,2,1,0:T(8,128)(2,1)S(1)}, bf16[2,1,512,128]{3,2,1,0:T(8,128)(2,1)}, u32[]{:S(2)}) copy-start(bf16[2,1,512,128]{3,2,1,0:T(8,128)(2,1)} %get-tuple-element.590) | copy-start | bytes 786436 | tf_op jit(solution)/shard_map/vmap()/while
  15.9 7.2 %copy-start.2 = (bf16[2,1,512,128]{3,2,1,0:T(8,128)(2,1)S(1)}, bf16[2,1,512,128]{3,2,1,0:T(8,128)(2,1)}, u32[]{:S(2)}) copy-start(bf16[2,1,512,128]{3,2,1,0:T(8,128)(2,1)} %get-tuple-element.591) | copy-start | bytes 786436 | tf_op jit(solution)/shard_map/vmap()/while
  23.7 17.8 %copy-start.9 = (f32[2,1,512,128]{3,2,1,0:T(8,128)}, f32[2,1,512,128]{3,2,1,0:T(8,128)S(1)}, u32[]{:S(2)}) copy-start(f32[2,1,512,128]{3,2,1,0:T(8,128)S(1)} %get-tuple-element.269) | copy-start | bytes 1572868
  23.7 17.8 %copy-start.10 = (f32[2,1,128,128]{3,2,1,0:T(8,128)}, f32[2,1,128,128]{3,2,1,0:T(8,128)S(1)}, u32[]{:S(2)}) copy-start(f32[2,1,128,128]{3,2,1,0:T(8,128)S(1)} %get-tuple-element.606) | copy-start | bytes 393220
  25.0 124.3 %all-to-all-start = ((bf16[32,1,1,128,128]{4,3,2,1,0:T(8,128)(2,1)}), bf16[32,1,1,128,128]{4,3,2,1,0:T(8,128)(2,1)}, u32[]{:S(2)}, u32[]{:S(2)}) async-start(bf16[32,1,1,128,128]{4,3,2,1,0:T(8,128)(2,1)} %stack.2), calls=%async_computation | async-start | bytes 2097152 | tf_op jit(solution)/shard_map/all_to_all | solution.py:138
  41.6 134.6 %reduce-scatter.4.cloned.1.call-start = ((), (), s32[]{:S(2)}) async-start(), calls=%async_computation.3 | async-start | bytes 1671168
  47.7 1.5 copy-start.13
  47.7 97.0 %copy-start.12 = (bf16[1,1024,128]{2,1,0:T(8,128)(2,1)S(1)}, bf16[1,1024,128]{2,1,0:T(8,128)(2,1)}, u32[]{:S(2)}) copy-start(bf16[1,1024,128]{2,1,0:T(8,128)(2,1)} %param.13) | copy-start | bytes 786436
  49.1 102.4 %copy-start.5 = (bf16[2,1,512,128]{3,2,1,0:T(8,128)(2,1)S(1)}, bf16[2,1,512,128]{3,2,1,0:T(8,128)(2,1)}, u32[]{:S(2)}) copy-start(bf16[2,1,512,128]{3,2,1,0:T(8,128)(2,1)} %get-tuple-element.644) | copy-start | bytes 786436
  49.1 252.3 %all-gather.3.cloned.1.call-start = ((), (), s32[]{:S(2)}) async-start(), calls=%async_computation.2 | async-start | bytes 1081344 | tf_op jit(solution)/shard_map/all_gather | solution.py:175
  149.3 3.2 %copy-start.14 = (f32[1024]{0:T(1024)}, f32[1024]{0:T(1024)S(1)}, u32[]{:S(2)}) copy-start(f32[1024]{0:T(1024)S(1)} %get-tuple-element.432) | copy-start | bytes 12292
  151.5 1.9 copy-start.1
  151.5 1.8 copy-start.3
  152.1 1.3 copy-start.16
  155.3 5.2 %copy-start.6 = (f32[2,1,512,128]{3,2,1,0:T(8,128)S(1)}, f32[2,1,512,128]{3,2,1,0:T(8,128)}, u32[]{:S(2)}) copy-start(f32[2,1,512,128]{3,2,1,0:T(8,128)} %get-tuple-element.612) | copy-start | bytes 1572868 | tf_op jit(solution)/shard_map/vmap()/while
  155.3 5.3 %copy-start.11 = (f32[2,1,128,128]{3,2,1,0:T(8,128)S(1)}, f32[2,1,128,128]{3,2,1,0:T(8,128)}, u32[]{:S(2)}) copy-start(f32[2,1,128,128]{3,2,1,0:T(8,128)} %get-tuple-element.634) | copy-start | bytes 393220 | tf_op jit(solution)/shard_map/vmap()/while
  160.9 3.5 %copy-start.7 = (f32[2,1,512,128]{3,2,1,0:T(8,128)}, f32[2,1,512,128]{3,2,1,0:T(8,128)S(1)}, u32[]{:S(2)}) copy-start(f32[2,1,512,128]{3,2,1,0:T(8,128)S(1)} %fusion.198) | copy-start | bytes 1572868 | tf_op jit(solution)/shard_map/vmap()/while
  166.3 5.2 %copy-start.6 = (f32[2,1,512,128]{3,2,1,0:T(8,128)S(1)}, f32[2,1,512,128]{3,2,1,0:T(8,128)}, u32[]{:S(2)}) copy-start(f32[2,1,512,128]{3,2,1,0:T(8,128)} %get-tuple-element.612) | copy-start | bytes 1572868 | tf_op jit(solution)/shard_map/vmap()/while
  166.3 5.3 %copy-start.11 = (f32[2,1,128,128]{3,2,1,0:T(8,128)S(1)}, f32[2,1,128,128]{3,2,1,0:T(8,128)}, u32[]{:S(2)}) copy-start(f32[2,1,128,128]{3,2,1,0:T(8,128)} %get-tuple-element.634) | copy-start | bytes 393220 | tf_op jit(solution)/shard_map/vmap()/while
  172.0 3.5 %copy-start.7 = (f32[2,1,512,128]{3,2,1,0:T(8,128)}, f32[2,1,512,128]{3,2,1,0:T(8,128)S(1)}, u32[]{:S(2)}) copy-start(f32[2,1,512,128]{3,2,1,0:T(8,128)S(1)} %fusion.198) | copy-start | bytes 1572868 | tf_op jit(solution)/shard_map/vmap()/while
  175.5 4.4 %copy-start.8 = (f32[2,1,512,128]{3,2,1,0:T(8,128)S(1)}, f32[2,1,512,128]{3,2,1,0:T(8,128)}, u32[]{:S(2)}) copy-start(f32[2,1,512,128]{3,2,1,0:T(8,128)} %get-tuple-element.272) | copy-start | bytes 1572868
  175.5 4.4 %copy-start.15 = (f32[1024]{0:T(1024)S(1)}, f32[1024]{0:T(1024)}, u32[]{:S(2)}) copy-start(f32[1024]{0:T(1024)} %copy-done.14) | copy-start | bytes 12292
  175.5 126.0 %copy-start.17 = (f32[32]{0:T(128)S(1)}, f32[32]{0:T(128)}, u32[]{:S(2)}) copy-start(f32[32]{0:T(128)} %get-tuple-element.387) | copy-start | bytes 388
Sparse Core Ops, SparseCore 0:
  49.3 92.4 reduce-scatter.3
Sparse Core Ops, SparseCore 1:
  176.2 125.2 all-gather.2
